TPU v7x, 512 devices: a whole 4x8x8 slice. The times are simulated.
512 devices in a mesh: pos: 64 (over z, y_lo, x), head: 8 (over y_hi, core).
Axes of the slice: x: 4, y: 8 (y_hi: 4, y_lo: 2; y = y_hi * 2 + y_lo), z: 8, core: 2. Of those that a mesh axis runs over, the one named last changes fastest.
Arguments:
- token_ids: int32 [65536], P('pos'), may hold values from 0 to 255
- token_table: float32 [256, 1024], replicated, may hold values from -6 to 6
- row_table: float32 [256, 1024], replicated, may hold values from -6 to 6
- col_table: float32 [256, 1024], replicated, may hold values from -6 to 6
- chan_table: float32 [3, 1024], replicated, may hold values from -6 to 6
- w_query: float32 [1024, 1024], P(None, 'head'), as said below
- w_key: float32 [1024, 1024], P(None, 'head'), as said below
- w_value: float32 [1024, 1024], P(None, 'head'), may hold values from -0.1875 to 0.1875
- w_out: float32 [1024, 1024], P('head', 'pos'), may hold values from -0.1875 to 0.1875
- w_in: float32 [1024, 4096], P('pos', 'head'), may hold values from -0.1875 to 0.1875
- w_down: float32 [4096, 1024], P('head', 'pos'), may hold values from -0.09375 to 0.09375
Outputs:
- latent_out: float32 [512, 1024], P('pos')
Inputs may be any that keep to these rules, and one draw needn't show every extreme that they name: `w_query`: entries of order 1024^-0.5 times a few. `w_key`: entries of order 1024^-0.5 times a few, or larger.
All inputs are finite; a program needn't handle non-finite values.
Results may differ from a plain program's by a relative error of at most 0.0003.
Values sent between devices are 32-bit elements; how exact they have to be, the bound alone decides.
No kernel may reach another device: no remote copies, remote signals or barrier semaphores. Data moves between devices by JAX's collectives and lax.ppermute only.
A program may use at most 128 MiB of HBM per device.

v0:
```python
import jax
import jax.numpy as jnp
from jax import lax
from jax.sharding import PartitionSpec as P

HD = 64
IMG = 256
LAT = 512


def broadcast(shard, axis, root):
    mine = lax.axis_index(axis) == root
    return lax.psum(jnp.where(mine, shard, jnp.zeros_like(shard)), axis)


def combined_all(value, axis, join):
    pieces = jax.tree.map(lambda part: lax.all_gather(part, axis), value)
    head = jax.tree.map(lambda part: part[0], pieces)
    tail = jax.tree.map(lambda part: part[1:], pieces)
    so_far, _ = lax.scan(lambda so_far, piece: (join(so_far, piece), None), head, tail)
    return so_far


def layer_norm(values):
    center = values - jnp.mean(values, axis=-1, keepdims=True)
    spread = jnp.mean(center * center, axis=-1, keepdims=True)
    return center * lax.rsqrt(spread + 1e-05)


def embed(ids, where, tables):
    token_table, row_table, col_table, chan_table = tables
    channel = where % 3
    pixel = where // 3
    summed = jnp.take(token_table, ids, axis=0) + jnp.take(row_table, pixel // IMG, axis=0)
    summed = (
        summed + jnp.take(col_table, pixel % IMG, axis=0) + jnp.take(chan_table, channel, axis=0)
    )
    return layer_norm(summed)


def merge_states(first, second):
    peak = jnp.maximum(first[0], second[0])
    left = jnp.exp(first[0] - peak)
    right = jnp.exp(second[0] - peak)
    weight = first[1] * left + second[1] * right
    accum = first[2] * left[..., None] + second[2] * right[..., None]
    return (peak, weight, accum)


def head_sum(partial_value):
    return lax.psum(partial_value, "head")


def per_device(
    token_ids,
    token_table,
    row_table,
    col_table,
    chan_table,
    w_query,
    w_key,
    w_value,
    w_out,
    w_in,
    w_down,
):
    highest = lax.Precision.HIGHEST
    tables = (token_table, row_table, col_table, chan_table)
    local = token_ids.shape[0]
    n_pos = lax.axis_size("pos")
    index = lax.axis_index("pos")
    total = local * n_pos
    heads_dev = w_key.shape[1] // HD
    key_block = min(512, local)
    lat_pos = total - LAT + jnp.arange(LAT)
    own_queries = jnp.dot(
        embed(token_ids[local - LAT :], lat_pos, tables), w_query, precision=highest
    )
    queries = broadcast(own_queries, "pos", n_pos - 1)
    queries = queries.reshape(LAT, heads_dev, HD).transpose(1, 0, 2) * HD ** (-0.5)

    def step(carry, start):
        top, weight, accum = carry
        where = index * local + start + jnp.arange(key_block)
        ids = lax.dynamic_slice_in_dim(token_ids, start, key_block)
        emb = embed(ids, where, tables)
        keys = jnp.dot(emb, w_key, precision=highest).reshape(key_block, heads_dev, HD)
        vals = jnp.dot(emb, w_value, precision=highest).reshape(key_block, heads_dev, HD)
        scores = jnp.einsum("hld,khd->hlk", queries, keys, precision=highest)
        scores = jnp.where(where[None, None, :] <= lat_pos[None, :, None], scores, -1e30)
        new_top = jnp.maximum(top, jnp.max(scores, axis=-1))
        factor = jnp.exp(top - new_top)
        probs = jnp.exp(scores - new_top[..., None])
        weight = weight * factor + jnp.sum(probs, axis=-1)
        accum = accum * factor[..., None] + jnp.einsum(
            "hlk,khd->hld", probs, vals, precision=highest
        )
        return ((new_top, weight, accum), None)

    starts = jnp.arange(local // key_block) * key_block
    init = (
        jnp.full((heads_dev, LAT), -1e30, jnp.float32),
        jnp.zeros((heads_dev, LAT), jnp.float32),
        jnp.zeros((heads_dev, LAT, HD), jnp.float32),
    )
    (top, weight, accum), _ = lax.scan(step, init, starts)
    lat_rows = LAT // n_pos
    top, weight, accum = combined_all((top, weight, accum), "pos", merge_states)
    weight = lax.dynamic_slice_in_dim(weight, index * lat_rows, lat_rows, 1)
    accum = lax.dynamic_slice_in_dim(accum, index * lat_rows, lat_rows, 1)
    attended = (accum / weight[..., None]).transpose(1, 0, 2).reshape(lat_rows, heads_dev * HD)
    whole_out, whole_in, whole_down = (
        lax.all_gather(w_out, "pos", axis=1, tiled=True),
        lax.all_gather(w_in, "pos", axis=0, tiled=True),
        lax.all_gather(w_down, "pos", axis=1, tiled=True),
    )
    projected = head_sum(jnp.dot(attended, whole_out, precision=highest))
    hidden = jax.nn.gelu(jnp.dot(layer_norm(projected), whole_in, precision=highest))
    return projected + head_sum(jnp.dot(hidden, whole_down, precision=highest))


def solution(mesh):
    placed = (
        P("pos"),
        P(),
        P(),
        P(),
        P(),
        P(None, "head"),
        P(None, "head"),
        P(None, "head"),
        P("head", "pos"),
        P("pos", "head"),
        P("head", "pos"),
    )
    return jax.shard_map(
        per_device, mesh=mesh, in_specs=placed, out_specs=P("pos", None), check_vma=False
    )
```

profile of v0, /device:TPU:2, one launch (start us, length us, event | category | flops | bytes accessed | tf_op | source)
XLA Modules:
  0.0 1644.0 jit_solution(15092672931124769)
XLA Ops:
  8.1 4.9 gather_fusion.4
  13.1 2.7 gather_fusion.5
  15.8 2.7 gather_fusion.6
  21.1 4.0 fusion.61
  26.8 4.3 fusion.34
  31.2 567.1 %all-reduce.2.cloned.1.call-done = f32[512,128]{1,0:T(8,128)} async-done(((f32[512,128]{1,0:T(8,128)}), f32[512,128]{1,0:T(8,128)}) %all-reduce.2.cloned.1.call-update) | async-done | bytes 262160 | tf_op jit(solution)/shard_map/psum | solution.py:13
  599.4 72.5 %while.33 = (s32[]{:T(128)}, f32[2,512]{1,0:T(2,128)S(1)}, f32[2,512]{1,0:T(2,128)S(1)}, f32[2,512,64]{1,2,0:T(8,128)}, s32[2]{0:T(128)S(1)}, /*index=5*/s32[]{:...) while((s32[]{:T(128)}, f32[2,512]{1,0:T(2,128)S(1)}, ...), condition=%wide.region_8.11_spmd.clone, body=%wide.region_3.0_spmd.clone.sunk | while | flops 2427988480 | bytes 55456068 | solution.py:106
  603.1 2.7 gather_fusion.3
  605.8 2.6 gather_fusion
  608.4 4.8 gather_fusion.1
  613.3 2.7 gather_fusion.2
  616.0 4.0 fusion.101
  621.0 3.2 fusion.107
  627.0 3.4 fusion.103
  638.7 2.7 gather_fusion.3
  644.1 4.8 gather_fusion.1
  649.0 2.7 gather_fusion.2
  651.7 4.0 fusion.101
  656.7 3.2 fusion.107
  662.7 3.4 fusion.103
  668.4 3.6 fusion.108
  673.3 155.9 %all_gather.33 = f32[128,1024]{0,1:T(8,128)S(1)} all-gather(f32[128,16]{0,1:T(8,128)S(1)} %copy-done.12), channel_id=1, replica_groups=mesh['pos'=64,'head'=8] {'pos'}, dimensions={1}, use_global_device_ids=true | all-gather | bytes 532480 | tf_op jit(solution)/shard_map/all_gather | solution.py:113
  829.2 153.3 %all-gather.4 = f32[64,2,512]{2,1,0:T(2,128)S(1)} all-gather(f32[1,2,512]{2,1,0:T(2,128)S(1)} %bitcast.83), channel_id=3, replica_groups=mesh['pos'=64,'head'=8] {'pos'}, dimensions={0}, use_global_device_ids=true | all-gather | bytes 266240 | tf_op jit(solution)/shard_map/all_gather | solution.py:17
  982.5 151.4 %all-gather.3 = f32[64,2,512]{2,1,0:T(2,128)S(1)} all-gather(f32[1,2,512]{2,1,0:T(2,128)S(1)} %bitcast.82), channel_id=2, replica_groups=mesh['pos'=64,'head'=8] {'pos'}, dimensions={0}, use_global_device_ids=true | all-gather | bytes 266240 | tf_op jit(solution)/shard_map/all_gather | solution.py:17
  1135.1 12.2 slice.59
  1147.3 106.7 %while.32 = (s32[]{:T(128)}, f32[2,512]{1,0:T(2,128)S(1)}, f32[2,512]{1,0:T(2,128)S(1)}, f32[2,512,64]{2,1,0:T(8,128)S(1)}, f32[63,2,512]{2,1,0:T(2,128)S(1)}, /...) while((s32[]{:T(128)}, f32[2,512]{1,0:T(2,128)S(1)}, f32[2,512]{1,0:T(2,128)S(1)}, ...), condition=%wide.region_10.13_spmd, body=%wide.region_9.12_spmd.sunk | while | flops 202754 | bytes 1876061 | solution.py:20
  1254.8 27.2 %psum.22 = f32[8,1024]{1,0:T(8,128)S(1)} all-reduce(f32[8,1024]{1,0:T(8,128)S(1)} %fusion.62), channel_id=1, replica_groups=mesh['pos'=64,'head'=8] {'head'}, use_global_device_ids=true, to_apply=%region_11.14 | all-reduce | flops 8192 | bytes 65536 | tf_op jit(solution)/shard_map/psum | solution.py:51
  1282.3 22.3 %all-gather.9.cloned.1.call-done = f32[1024,512]{1,0:T(8,128)} async-done(((f32[16,512]{1,0:T(8,128)}), f32[1024,512]{1,0:T(8,128)}) %all-gather.9.cloned.1.call-update) | async-done | bytes 2097168 | tf_op jit(solution)/shard_map/all_gather | solution.py:114
  1304.6 2.7 fusion.48
  1307.3 298.9 %all-gather.11.cloned.1.call-done = f32[512,1024]{0,1:T(8,128)} async-done(((f32[512,16]{0,1:T(8,128)}), f32[512,1024]{0,1:T(8,128)}) %all-gather.11.cloned.1.call-update) | async-done | bytes 2097168 | tf_op jit(solution)/shard_map/all_gather | solution.py:115
  1606.2 3.4 fusion.63
  1609.6 27.2 %psum.23 = f32[8,1024]{1,0:T(8,128)S(1)} all-reduce(f32[8,1024]{1,0:T(8,128)S(1)} %fusion.63), channel_id=1, replica_groups=mesh['pos'=64,'head'=8] {'head'}, use_global_device_ids=true, to_apply=%region_14.17 | all-reduce | flops 8192 | bytes 65536 | tf_op jit(solution)/shard_map/psum | solution.py:51
  (369 shorter events, 135.1 us)
Async XLA Ops:
  6.5 20.2 %copy-start = (f32[1024,128]{1,0:T(8,128)S(1)}, f32[1024,128]{1,0:T(8,128)}, u32[]{:S(2)}) copy-start(f32[1024,128]{1,0:T(8,128)} %param.24) | copy-start | bytes 1572868
  6.5 591.7 %all-reduce.2.cloned.1.call-start = ((), (), s32[]{:S(2)}) async-start(), calls=%async_computation | async-start | bytes 524288 | tf_op jit(solution)/shard_map/psum | solution.py:13
  8.1 5.0 copy-start.4
  13.1 2.7 copy-start.5
  15.8 2.7 copy-start.2
  25.0 1.3 copy-start.7
  26.7 572.6 %copy-start.3 = (f32[256,1024]{1,0:T(8,128)S(1)}, f32[256,1024]{1,0:T(8,128)}, u32[]{:S(2)}) copy-start(f32[256,1024]{1,0:T(8,128)} %param.20) | copy-start | bytes 3145732
  26.8 572.6 %copy-start.8 = (f32[1024,128]{1,0:T(8,128)S(1)}, f32[1024,128]{1,0:T(8,128)}, u32[]{:S(2)}) copy-start(f32[1024,128]{1,0:T(8,128)} %param.25) | copy-start | bytes 1572868
  26.8 572.6 %copy-start.11 = (s32[1024]{0:T(1024)S(1)}, s32[1024]{0:T(1024)}, u32[]{:S(2)}) copy-start(s32[1024]{0:T(1024)} %param.19) | copy-start | bytes 12292
  31.1 1102.9 %all-gather.13.cloned.1.call-start = ((), (), s32[]{:S(2)}) async-start(), calls=%async_computation.3 | async-start | bytes 17039360 | tf_op jit(solution)/shard_map/all_gather | solution.py:17
  599.4 73.9 %copy-start.12 = (f32[128,16]{0,1:T(8,128)S(1)}, f32[128,16]{0,1:T(8,128)}, u32[]{:S(2)}) copy-start(f32[128,16]{0,1:T(8,128)} %param.27) | copy-start | bytes 24580
  620.0 1.0 copy-start.9
  630.4 2.2 copy-start.10
  630.4 2.3 copy-start.6
  655.7 1.0 copy-start.9
  666.1 2.2 copy-start.10
  666.1 2.3 copy-start.6
  672.0 632.7 %all-gather.9.cloned.1.call-start = ((), (), s32[]{:S(2)}) async-start(), calls=%async_computation.1 | async-start | bytes 2129920 | tf_op jit(solution)/shard_map/all_gather | solution.py:114
  672.7 933.5 %all-gather.11.cloned.1.call-start = ((), (), s32[]{:S(2)}) async-start(), calls=%async_computation.2 | async-start | bytes 2129920 | tf_op jit(solution)/shard_map/all_gather | solution.py:115
  1282.3 355.2 %copy-start.1 = (f32[1024,128]{1,0:T(8,128)S(1)}, f32[1024,128]{1,0:T(8,128)}, u32[]{:S(2)}) copy-start(f32[1024,128]{1,0:T(8,128)} %param.24) | copy-start | bytes 1572868
Sparse Core Ops, SparseCore 0:
  31.2 567.0 all-reduce.1
  672.1 330.5 all-gather.12
  1004.8 299.7 all-gather.8
  1306.6 299.6 all-gather.10
where the time goes:
time: 1650 us; the launch traced here: 1640 us
  waiting for transfers between devices  890 us (54%)
  blocking collectives  515 us (31%)
  local copies, waits for them, and re-layouts  130 us (8%)
  other arithmetic  52.8 us (3%)
  matrix products  35.3 us (2%)
    psum x1, waiting for transfers between devices, broadcast(): return lax.psum(jnp.where(mine, shard, jnp.zeros_like(shard)), axis)  567 us
    all_gather x2, blocking collectives, combined_all(): pieces = jax.tree.map(lambda part: lax.all_gather(part, axis), value)  305 us
    all_gather x1, waiting for transfers between devices, per_device(): lax.all_gather(w_down, 'pos', axis=1, tiled=True)  299 us
    all_gather x1, blocking collectives, per_device(): lax.all_gather(w_out, 'pos', axis=1, tiled=True)  156 us
    dynamic_slice x126, local copies, waits for them, and re-layouts, combined_all(): lax.scan(lambda so_far, piece: (join(so_far, piece), None), head, tail)  73.7 us
    psum x2, blocking collectives, head_sum(): return lax.psum(partial_value, 'head')  54.4 us
  transfers between devices with their start and end apart: 4, of which 3 were waited for; matrix products, arithmetic and copies ran while one was open for 7% of the time, Pallas kernels for 0%

commit v1 on v0

--- a/solution.py
+++ b/solution.py
@@ -10,7 +10,7 @@
 
 def broadcast(shard, axis, root):
     mine = lax.axis_index(axis) == root
-    return lax.psum(jnp.where(mine, shard, jnp.zeros_like(shard)), axis)
+    return lax.all_gather(jnp.where(mine, shard, jnp.zeros_like(shard)), axis).sum(axis=0)
 
 
 def combined_all(value, axis, join):

time: 1650 us -> 1420 us (0.86)
  waiting for transfers between devices: 890 us -> 654 us
    psum x1 -> x0, waiting for transfers between devices: 567 us -> none  [broadcast(): return lax.psum(jnp.where(mine, shard, jnp.zeros_like(shard)), axis)]
    all_gather x0 -> x1, waiting for transfers between devices: none -> 335 us  [broadcast(): lax.all_gather(jnp.where(mine, shard, jnp.zeros_like(shard)), axis)]
  transfers between devices with their start and end apart: 4 -> 4, of which waited for: 3 -> 3; matrix products, arithmetic and copies ran while one was open for 7% -> 9% of each run, Pallas kernels for 0% -> 0%
where the time goes in v1:
time: 1420 us
  waiting for transfers between devices  654 us (46%)
  blocking collectives  517 us (36%)
  local copies, waits for them, and re-layouts  129 us (9%)
  other arithmetic  58.5 us (4%)
  matrix products  37.2 us (3%)
    all_gather x1, waiting for transfers between devices, broadcast(): lax.all_gather(jnp.where(mine, shard, jnp.zeros_like(shard)), axis)  335 us
    all_gather x2, blocking collectives, combined_all(): pieces = jax.tree.map(lambda part: lax.all_gather(part, axis), value)  308 us
    all_gather x1, waiting for transfers between devices, per_device(): lax.all_gather(w_down, 'pos', axis=1, tiled=True)  299 us
    all_gather x1, blocking collectives, per_device(): lax.all_gather(w_out, 'pos', axis=1, tiled=True)  154 us
    dynamic_slice x126, local copies, waits for them, and re-layouts, combined_all(): lax.scan(lambda so_far, piece: (join(so_far, piece), None), head, tail)  73.7 us
    psum x2, blocking collectives, head_sum(): return lax.psum(partial_value, 'head')  54.4 us
    add x63, other arithmetic, merge_states(): accum = first[2] * left[..., None] + second[2] * right[..., None]  29.1 us
  transfers between devices with their start and end apart: 4, of which 3 were waited for; matrix products, arithmetic and copies ran while one was open for 9% of the time, Pallas kernels for 0%

profile of v1, /device:TPU:2, one launch (start us, length us, event | category | flops | bytes accessed | tf_op | source)
XLA Modules:
  0.0 1416.9 jit_solution(8872194852928733295)
XLA Ops:
  8.1 4.9 gather_fusion.4
  13.1 2.7 gather_fusion.5
  15.8 2.7 gather_fusion.6
  21.1 4.0 fusion.61
  26.7 4.2 fusion.34
  31.0 334.8 %all-gather.15.cloned.1.call-done = f32[32768,128]{1,0:T(8,128)} async-done(((f32[512,128]{1,0:T(8,128)}), f32[32768,128]{1,0:T(8,128)}) %all-gather.15.cloned.1.call-update) | async-done | bytes 16777232 | tf_op jit(solution)/shard_map/all_gather | solution.py:13
  365.8 6.7 reduce_sum.86
  372.7 73.4 %while.33 = (s32[]{:T(128)}, f32[2,512]{1,0:T(2,128)S(1)}, f32[2,512]{1,0:T(2,128)S(1)}, f32[2,512,64]{1,2,0:T(8,128)}, s32[2]{0:T(128)S(1)}, /*index=5*/s32[]{:...) while((s32[]{:T(128)}, f32[2,512]{1,0:T(2,128)S(1)}, ...), condition=%wide.region_8.11_spmd.clone, body=%wide.region_3.0_spmd.clone.sunk | while | flops 2427988480 | bytes 53358888 | solution.py:106
  376.4 2.7 gather_fusion.3
  381.7 4.8 gather_fusion.1
  386.6 2.7 gather_fusion.2
  389.3 4.0 fusion.101
  393.7 4.3 fusion.107
  400.7 3.4 fusion.103
  412.5 2.7 gather_fusion.3
  417.8 4.8 gather_fusion.1
  422.7 2.7 gather_fusion.2
  425.4 4.0 fusion.101
  429.8 4.3 fusion.107
  436.8 3.4 fusion.103
  442.5 3.5 fusion.108
  447.4 154.0 %all_gather.41 = f32[128,1024]{0,1:T(8,128)S(1)} all-gather(f32[128,16]{0,1:T(8,128)S(1)} %copy-done.11), channel_id=1, replica_groups=mesh['pos'=64,'head'=8] {'pos'}, dimensions={1}, use_global_device_ids=true | all-gather | bytes 532480 | tf_op jit(solution)/shard_map/all_gather | solution.py:113
  601.3 157.1 %all-gather.5 = f32[64,2,512]{2,1,0:T(2,128)S(1)} all-gather(f32[1,2,512]{2,1,0:T(2,128)S(1)} %bitcast.85), channel_id=4, replica_groups=mesh['pos'=64,'head'=8] {'pos'}, dimensions={0}, use_global_device_ids=true | all-gather | bytes 266240 | tf_op jit(solution)/shard_map/all_gather | solution.py:17
  758.5 151.2 %all-gather.4 = f32[64,2,512]{2,1,0:T(2,128)S(1)} all-gather(f32[1,2,512]{2,1,0:T(2,128)S(1)} %bitcast.84), channel_id=3, replica_groups=mesh['pos'=64,'head'=8] {'pos'}, dimensions={0}, use_global_device_ids=true | all-gather | bytes 266240 | tf_op jit(solution)/shard_map/all_gather | solution.py:17
  911.0 12.2 slice.59
  923.2 106.6 %while.32 = (s32[]{:T(128)}, f32[2,512]{1,0:T(2,128)S(1)}, f32[2,512]{1,0:T(2,128)S(1)}, f32[2,512,64]{2,1,0:T(8,128)S(1)}, f32[63,2,512]{2,1,0:T(2,128)S(1)}, /...) while((s32[]{:T(128)}, f32[2,512]{1,0:T(2,128)S(1)}, f32[2,512]{1,0:T(2,128)S(1)}, ...), condition=%wide.region_10.13_spmd, body=%wide.region_9.12_spmd.sunk | while | flops 202754 | bytes 1876061 | solution.py:20
  1030.6 27.2 %psum.14 = f32[8,1024]{1,0:T(8,128)S(1)} all-reduce(f32[8,1024]{1,0:T(8,128)S(1)} %fusion.62), channel_id=1, replica_groups=mesh['pos'=64,'head'=8] {'head'}, use_global_device_ids=true, to_apply=%region_11.14 | all-reduce | flops 8192 | bytes 65536 | tf_op jit(solution)/shard_map/psum | solution.py:51
  1058.2 19.6 %all-gather.11.cloned.1.call-done = f32[1024,512]{1,0:T(8,128)} async-done(((f32[16,512]{1,0:T(8,128)}), f32[1024,512]{1,0:T(8,128)}) %all-gather.11.cloned.1.call-update) | async-done | bytes 2097168 | tf_op jit(solution)/shard_map/all_gather | solution.py:114
  1077.8 2.7 fusion.48
  1080.5 298.7 %all-gather.13.cloned.1.call-done = f32[512,1024]{0,1:T(8,128)} async-done(((f32[512,16]{0,1:T(8,128)}), f32[512,1024]{0,1:T(8,128)}) %all-gather.13.cloned.1.call-update) | async-done | bytes 2097168 | tf_op jit(solution)/shard_map/all_gather | solution.py:115
  1379.1 3.4 fusion.63
  1382.5 27.2 %psum.15 = f32[8,1024]{1,0:T(8,128)S(1)} all-reduce(f32[8,1024]{1,0:T(8,128)S(1)} %fusion.63), channel_id=1, replica_groups=mesh['pos'=64,'head'=8] {'head'}, use_global_device_ids=true, to_apply=%region_14.17 | all-reduce | flops 8192 | bytes 65536 | tf_op jit(solution)/shard_map/psum | solution.py:51
  (366 shorter events, 135.5 us)
Async XLA Ops:
  6.5 20.2 %copy-start = (f32[1024,128]{1,0:T(8,128)S(1)}, f32[1024,128]{1,0:T(8,128)}, u32[]{:S(2)}) copy-start(f32[1024,128]{1,0:T(8,128)} %param.24) | copy-start | bytes 1572868
  6.5 359.3 %all-gather.15.cloned.1.call-start = ((), (), s32[]{:S(2)}) async-start(), calls=%async_computation.2 | async-start | bytes 17039360 | tf_op jit(solution)/shard_map/all_gather | solution.py:13
  8.1 5.0 copy-start.4
  13.1 2.7 copy-start.5
  15.8 2.7 copy-start.2
  25.0 1.3 copy-start.7
  30.9 878.9 %all-gather.17.cloned.1.call-start = ((), (), s32[]{:S(2)}) async-start(), calls=%async_computation.3 | async-start | bytes 17039360 | tf_op jit(solution)/shard_map/all_gather | solution.py:17
  365.8 6.8 copy-start.3
  365.8 6.8 copy-start.8
  365.8 6.8 copy-start.10
  372.7 74.7 %copy-start.11 = (f32[128,16]{0,1:T(8,128)S(1)}, f32[128,16]{0,1:T(8,128)}, u32[]{:S(2)}) copy-start(f32[128,16]{0,1:T(8,128)} %param.27) | copy-start | bytes 24580
  404.0 2.2 copy-start.9
  404.1 2.3 copy-start.6
  440.2 2.2 copy-start.9
  440.2 2.3 copy-start.6
  446.0 631.7 %all-gather.11.cloned.1.call-start = ((), (), s32[]{:S(2)}) async-start(), calls=%async_computation | async-start | bytes 2129920 | tf_op jit(solution)/shard_map/all_gather | solution.py:114
  446.8 932.3 %all-gather.13.cloned.1.call-start = ((), (), s32[]{:S(2)}) async-start(), calls=%async_computation.1 | async-start | bytes 2129920 | tf_op jit(solution)/shard_map/all_gather | solution.py:115
  1058.1 352.2 %copy-start.1 = (f32[1024,128]{1,0:T(8,128)S(1)}, f32[1024,128]{1,0:T(8,128)}, u32[]{:S(2)}) copy-start(f32[1024,128]{1,0:T(8,128)} %param.24) | copy-start | bytes 1572868
Sparse Core Ops, SparseCore 0:
  31.0 334.7 all-gather.14
  446.2 326.9 all-gather.16
  775.3 302.4 all-gather.10
  1079.7 299.3 all-gather.12
